TPU v7x, 32 devices: a whole 2x2x4 slice. The times are simulated.
32 devices in a mesh: dp: 8 (over y, x, core), expert: 4 (over z).
Axes of the slice: x: 2, y: 2, z: 4, core: 2. Of those that a mesh axis runs over, the one named last changes fastest.
Arguments:
- cotangent: bfloat16 [32768, 2048], P(('dp', 'expert')), may hold values from -6 to 6
- route_ids: int32 [32768, 6], P(('dp', 'expert')), may hold values from 0 to 63, all different within a row; in each aligned block of 1024 rows (0 to 1023, 1024 to 2047, ...) at most 192 rows name the same one
- route_weights: float32 [32768, 6], P(('dp', 'expert')), may hold values from 0.02 to 1
- hidden: bfloat16 [8, 6144, 1408], P('expert', 'dp'), may hold values from -6 to 6
- master: float32 [1408, 8, 2048], P('dp', 'expert'), may hold values from -0.3 to 0.3
- first_moment: float32 [1408, 8, 2048], P('dp', 'expert'), may hold values from -1.2 to 1.2
- second_moment: float32 [1408, 8, 2048], P('dp', 'expert'), may hold values from 0.002 to 0.05
Outputs:
- new_master: float32 [1408, 8, 2048], P('dp', 'expert')
- new_first: float32 [1408, 8, 2048], P('dp', 'expert')
- new_second: float32 [1408, 8, 2048], P('dp', 'expert')
Inputs may be any that keep to these rules, and one draw needn't show every extreme that they name: `route_ids`: each row names 6 different experts. Within the 1024 rows of one device no expert is named by more than 192 rows.
All inputs are finite; a program needn't handle non-finite values.
Results may differ from a plain program's by a relative error of at most 0.0019.
Values may be sent and summed in bfloat16 or wider, within the bound.
A program may use at most 128 MiB of HBM per device.

v0:
```python
import jax
import jax.numpy as jnp
from jax import lax
from jax.sharding import PartitionSpec as P

beta_one = 0.9
beta_two = 0.999
learning_rate = 0.001
epsilon = 1e-08
decay_rate = 0.1
step_count = 4.0


def slot_table(route_ids, route_weights, window, capacity, local_count, groups):
    tokens = route_ids.shape[0]
    onehot = (route_ids[:, :, None] == jnp.arange(window, dtype=jnp.int32)[None, None, :]).astype(
        jnp.int32
    )
    counts = jnp.sum(onehot, axis=1)
    before = jnp.cumsum(counts, axis=0) - counts
    ranks = jnp.sum(onehot * before[:, None, :], axis=2)
    inside = route_ids < window
    position = (
        route_ids % local_count * (groups * capacity) + route_ids // local_count * capacity + ranks
    )
    position = jnp.where(inside, position, window * capacity)
    anchor = jnp.broadcast_to(jnp.arange(tokens, dtype=jnp.int32)[:, None], route_ids.shape)
    slot_anchor = (
        jnp.zeros((window * capacity + 1,), jnp.int32)
        .at[position.reshape(-1)]
        .set(anchor.reshape(-1))
    )
    masked = jnp.where(inside, route_weights, jnp.zeros_like(route_weights))
    slot_weight = (
        jnp.zeros((window * capacity + 1,), route_weights.dtype)
        .at[position.reshape(-1)]
        .set(masked.reshape(-1))
    )
    return (slot_anchor[:-1], slot_weight[:-1])


def shards(cotangent, route_ids, route_weights, hidden, master, first_moment, second_moment):
    groups = lax.axis_size("expert")
    local_count = hidden.shape[0]
    capacity = hidden.shape[1] // groups
    width = cotangent.shape[1]
    window = local_count * groups
    owned_rows = master.shape[0]
    slot_anchor, slot_weight = slot_table(
        route_ids, route_weights, window, capacity, local_count, groups
    )
    scaled = (cotangent[slot_anchor].astype(jnp.float32) * slot_weight[:, None]).astype(
        jnp.bfloat16
    )
    scaled = scaled.reshape(local_count, groups * capacity, width)
    received = lax.all_to_all(scaled, "expert", split_axis=1, concat_axis=1, tiled=True)
    pieces = []
    for expert_local in range(local_count):
        hidden_one = hidden[expert_local]
        received_one = received[expert_local]

        def one_term(start, count, hidden_one=hidden_one, received_one=received_one):
            return jnp.einsum(
                "rf,rd->fd", hidden_one, received_one, preferred_element_type=jnp.float32
            )

        pieces.append(
            lax.psum_scatter(
                one_term(jnp.int32(0), owned_rows * lax.axis_size("dp")),
                "dp",
                scatter_dimension=0,
                tiled=True,
            )
        )
    summed = jnp.stack(pieces, axis=1)
    gradient = summed / jnp.sqrt(jnp.float32(groups * capacity))
    new_first = beta_one * first_moment + (1.0 - beta_one) * gradient
    new_second = beta_two * second_moment + (1.0 - beta_two) * gradient * gradient
    corrected_first = new_first / (1.0 - beta_one**step_count)
    corrected_second = new_second / (1.0 - beta_two**step_count)
    update = corrected_first / (jnp.sqrt(corrected_second) + epsilon) + decay_rate * master
    new_master = master - learning_rate * update
    return (new_master, new_first, new_second)


def solution(mesh):
    placed = (
        P(("dp", "expert"), None),
        P(("dp", "expert"), None),
        P(("dp", "expert"), None),
        P("expert", "dp", None),
        P("dp", "expert", None),
        P("dp", "expert", None),
        P("dp", "expert", None),
    )
    return jax.shard_map(
        shards,
        mesh=mesh,
        in_specs=placed,
        out_specs=(P("dp", "expert", None), P("dp", "expert", None), P("dp", "expert", None)),
        check_vma=False,
    )
```

profile of v0, /device:TPU:0, one launch (start us, length us, event | category | flops | bytes accessed | tf_op | source)
XLA Modules:
  0.0 474.1 jit_solution(2417612220993016401)
XLA Ops:
  7.2 0.8 convert_reduce_fusion
  8.0 2.3 reduce-window.6
  10.8 0.8 select_reduce_fusion
  11.7 0.8 fusion.10
  12.5 0.8 broadcast_select_fusion
  13.5 0.3 reshape.92
  14.0 0.4 reshape.68
  14.5 23.0 %scatter_custom_fusion.1 = f32[1537]{0:T(1024)S(1)} fusion(s32[6144]{0:T(1024)S(1)} %bitcast.45, f32[6144]{0:T(1024)S(1)} %reshape.92, f32[]{:T(128)} %constant.62.clone.1), kind=kCustom, calls=%fused_computation.46 | custom fusion | bytes 6152 | tf_op jit(solution)/shard_map/scatter | solution.py:37
  37.8 23.0 %scatter_custom_fusion = s32[1537]{0:T(1024)S(1)} fusion(s32[6144]{0:T(1024)S(1)} %bitcast.46, s32[6144]{0:T(1024)S(1)} %reshape.84, s32[]{:T(128)} %constant.29.clone.1), kind=kCustom, calls=%fused_computation.48 | custom fusion | bytes 6152 | tf_op jit(solution)/shard_map/scatter | solution.py:31
  60.9 15.5 %gather_fusion = bf16[1536,2048]{1,0:T(8,128)(2,1)} fusion(bf16[1024,2048]{1,0:T(8,128)(2,1)} %param.7, s32[2048]{0:T(1024)S(1)} %pad_clamp_fusion), kind=kCustom, calls=%fused_computation | custom fusion | bytes 12589056 | tf_op jit(solution)/shard_map/gather | solution.py:52
  76.3 3.9 fusion
  80.2 13.0 %copy.75 = bf16[2,768,2048]{2,0,1:T(2,128)(2,1)S(1)} copy(bf16[2,768,2048]{2,1,0:T(8,128)(2,1)S(1)} %fusion) | data formatting | bytes 12582912 | tf_op jit(solution)/shard_map/convert_element_type | solution.py:52
  93.3 144.5 %all_to_all.5 = bf16[2,768,2048]{2,0,1:T(2,128)(2,1)S(1)} all-to-all(bf16[2,768,2048]{2,0,1:T(2,128)(2,1)S(1)} %copy.75), channel_id=1, replica_groups=mesh['dp'=8,'expert'=4] {'expert'}, dimensions={1} | all-to-all | bytes 12582912 | tf_op jit(solution)/shard_map/all_to_all | solution.py:56
  237.7 9.7 %fusion.23 = (bf16[1,768,2048]{2,0,1:T(2,128)(2,1)S(1)}, bf16[1,768,2048]{2,0,1:T(2,128)(2,1)}) fusion(bf16[2,768,2048]{2,0,1:T(2,128)(2,1)S(1)} %all_to_all.5), kind=kLoop, calls=%fused_computation.50 | loop fusion | bytes 12582912 | tf_op jit(solution)/shard_map/slice | solution.py:60
  247.5 9.6 %convolution_bitcast_fusion.1 = f32[1408,2048]{0,1:T(8,128)} fusion(bf16[1,768,2048]{2,0,1:T(2,128)(2,1)S(1)} %get-tuple-element.24, bf16[2,768,1408]{2,1,0:T(8,128)(2,1)S(1)} %bitcast.49), kind=kOutput, calls=%fused_computation.6 | convolution fusion | flops 4429185024 | bytes 19988480 | tf_op jit(solution)/shard_map/rf,rd->fd/dot_general | solution.py:63
  257.1 12.0 %copy.86 = f32[1408,2048]{1,0:T(8,128)} copy(f32[1408,2048]{0,1:T(8,128)} %convolution_bitcast_fusion.1) | data formatting | bytes 23068672
  269.2 12.6 %convolution_bitcast_fusion = f32[1408,2048]{0,1:T(8,128)} fusion(bf16[1,768,2048]{2,0,1:T(2,128)(2,1)} %get-tuple-element.25, bf16[2,768,1408]{2,1,0:T(8,128)(2,1)} %param.10), kind=kOutput, calls=%fused_computation.5 | convolution fusion | flops 4429185024 | bytes 19988480 | tf_op jit(solution)/shard_map/rf,rd->fd/dot_general | solution.py:63
  281.8 12.8 %copy.88 = f32[1408,2048]{1,0:T(8,128)} copy(f32[1408,2048]{0,1:T(8,128)} %convolution_bitcast_fusion) | data formatting | bytes 23068672
  294.6 61.4 %reduce-scatter.7.cloned.1.call-done = f32[176,2048]{1,0:T(8,128)} async-done(((f32[1408,2048]{1,0:T(8,128)}), f32[176,2048]{1,0:T(8,128)}) %reduce-scatter.7.cloned.1.call-update) | async-done | bytes 1441808 | tf_op jit(solution)/shard_map/reduce_scatter | solution.py:68
  356.0 90.7 %reduce-scatter.9.cloned.1.call-done = f32[176,2048]{1,0:T(8,128)} async-done(((f32[1408,2048]{1,0:T(8,128)}), f32[176,2048]{1,0:T(8,128)}) %reduce-scatter.9.cloned.1.call-update) | async-done | bytes 1441808 | tf_op jit(solution)/shard_map/reduce_scatter | solution.py:68
  446.7 9.2 %multiply_subtract_fusion = (f32[176,2,2048]{2,0,1:T(8,128)S(1)}, f32[176,2,2048]{2,0,1:T(8,128)S(1)}, f32[176,2,2048]{2,0,1:T(8,128)S(1)}) fusion(f32[176,2,2048]{2,1,0:T(2,128)S(1)} %copy-done, f32[176,1,2048]{2,0,1:T(8,128)} %bitcast.42, f32[176,1,2048]{2,0,1:T(8,128)} %bitcast.41, f32[176,2,2048]{2,1,0:T(2,128)} %param.12, f32[176,2,2048]{2,1,0:T(2,128)} %param.13), kind=kLoop, calls=%fused_computation.14 | loop fusion | flops 12255232 | bytes 20185088 | tf_op jit(solution)/shard_map/sub | solution.py:82
  455.9 3.8 copy.83
  459.7 3.8 copy.84
  463.5 3.8 copy.85
  (24 shorter events, 1.5 us)
Async XLA Ops:
  7.2 348.8 %reduce-scatter.7.cloned.1.call-start = ((), (), s32[]{:S(2)}) async-start(), calls=%async_computation.3 | async-start | bytes 12976128 | tf_op jit(solution)/shard_map/reduce_scatter | solution.py:68
  93.2 154.2 %slice-start = ((s8[4325376]{0:T(1024)(128)(4,1)}), s8[4194304]{0:T(1024)(128)(4,1)S(1)}, s32[]{:S(2)}) async-start(s8[4325376]{0:T(1024)(128)(4,1)} %bitcast.48), calls=%async_computation.5 | async-start | bytes 8388608
  237.7 9.7 %slice-start.1 = ((s8[4325376]{0:T(1024)(128)(4,1)}), s8[131072]{0:T(1024)(128)(4,1)S(1)}, s32[]{:S(2)}) async-start(s8[4325376]{0:T(1024)(128)(4,1)} %bitcast.48), calls=%async_computation.6 | async-start | bytes 262144
  269.2 177.5 %reduce-scatter.9.cloned.1.call-start = ((), (), s32[]{:S(2)}) async-start(), calls=%async_computation.4 | async-start | bytes 12976128 | tf_op jit(solution)/shard_map/reduce_scatter | solution.py:68
  294.6 152.1 %copy-start = (f32[176,2,2048]{2,1,0:T(2,128)S(1)}, f32[176,2,2048]{2,1,0:T(2,128)}, u32[]{:S(2)}) copy-start(f32[176,2,2048]{2,1,0:T(2,128)} %param.11) | copy-start | bytes 8650756
Sparse Core Ops, SparseCore 0:
  269.3 86.6 reduce-scatter.6
  359.5 87.1 reduce-scatter.8
where the time goes:
time: 475 us; the launch traced here: 474 us
  waiting for transfers between devices  152 us (32%)
  blocking collectives  144 us (30%)
  local copies, waits for them, and re-layouts  122 us (26%)
  matrix products  22.2 us (5%)
  other arithmetic  18.9 us (4%)
  between operations  14.2 us (3%)
    reduce_scatter x2, waiting for transfers between devices, shards(): lax.psum_scatter(one_term(jnp.int32(0), owned_rows * lax.axis_size('dp'))...  152 us
    all_to_all x1, blocking collectives, shards(): lax.all_to_all(scaled, 'expert', split_axis=1, concat_axis=1, tiled=True)  144 us
    unnamed x11, local copies, waits for them, and re-layouts  36.2 us
    scatter x1, local copies, waits for them, and re-layouts, slot_table(): slot_weight = jnp.zeros((window * capacity + 1,), route_weights.dtype).at...  23 us
    scatter x1, local copies, waits for them, and re-layouts, slot_table(): slot_anchor = jnp.zeros((window * capacity + 1,), jnp.int32).at[position....  23 us
    dot_general x2, matrix products, one_term(): jnp.einsum('rf,rd->fd', hidden_one, received_one, preferred_element_type=...  22.2 us
    gather x1, local copies, waits for them, and re-layouts, shards(): cotangent[slot_anchor].astype(jnp.float32) * slot_weight[:, None]  15.5 us
    convert_element_type x1, local copies, waits for them, and re-layouts, shards(): (cotangent[slot_anchor].astype(jnp.float32) * slot_weight[:, None]).astyp...  13 us
  transfers between devices with their start and end apart: 2, of which 2 were waited for; matrix products, arithmetic and copies ran while one was open for 5% of the time, Pallas kernels for 0%

commit v1 on v0

v1 whole, which is shorter than its diff:
```python
import functools

import jax
import jax.numpy as jnp
from jax import lax
from jax.experimental import pallas as pl
from jax.experimental.pallas import tpu as pltpu
from jax.sharding import PartitionSpec as P

beta_one = 0.9
beta_two = 0.999
learning_rate = 0.001
epsilon = 1e-08
decay_rate = 0.1
step_count = 4.0

MESH = pl.DeviceIdType.MESH
LANES = 128
CHUNK = 256


def gradient_kernel(
    dp,
    groups,
    ids_ref,
    weights_ref,
    cot_hbm,
    hidden_hbm,
    grad_ref,
    cot,
    hidden,
    turned,
    onehot,
    slot_weight,
    send,
    recv,
    part,
    pair_recv,
    peer_recv,
    own_sum,
    load_sem,
    send_sem,
    recv_sem,
    pair_sem,
    peer_send_sem,
    peer_recv_sem,
):
    d = lax.axis_index("dp")
    s = lax.axis_index("expert")
    half = dp // 2
    parity = lax.rem(d, 2)
    q = d // 2
    partner = d + 1 - 2 * parity
    chunks, width = recv.shape[0], recv.shape[-1]
    local_count, capacity = recv.shape[2], recv.shape[3]
    top, tokens = ids_ref.shape
    rows = groups * capacity
    own = grad_ref.shape[1]
    hidden_units = turned.shape[1]

    load_cot = pltpu.make_async_copy(cot_hbm, cot, load_sem.at[0])
    load_hidden = pltpu.make_async_copy(hidden_hbm, hidden, load_sem.at[1])
    load_cot.start()
    load_hidden.start()

    barrier = pltpu.get_barrier_semaphore()
    for j in range(1, groups):
        pl.semaphore_signal(
            barrier, inc=1, device_id=(d, lax.rem(s + j, groups)), device_id_type=MESH
        )
    pl.semaphore_signal(barrier, inc=1, device_id=(partner, s), device_id_type=MESH)
    for j in range(1, half):
        pl.semaphore_signal(
            barrier,
            inc=1,
            device_id=(lax.rem(q + j, half) * 2 + parity, s),
            device_id_type=MESH,
        )

    window = groups * local_count
    ids = ids_ref[...]
    weights = weights_ref[...]
    lane = lax.broadcasted_iota(jnp.int32, (window, tokens), 1)
    chosen, picked = [], []
    for k in range(window):
        hit = ids == k
        chosen.append(jnp.sum(hit.astype(jnp.int32), axis=0, keepdims=True))
        picked.append(jnp.sum(jnp.where(hit, weights, 0.0), axis=0, keepdims=True))
    count = jnp.concatenate(chosen, axis=0)
    total = count
    shift = 1
    while shift < tokens:
        total = total + jnp.where(lane >= shift, pltpu.roll(total, shift, 1), 0)
        shift *= 2
    rank = jnp.where(count > 0, total - count, -1)
    for k in range(window):
        group, local = k // local_count, k % local_count
        slot = lax.broadcasted_iota(jnp.int32, (capacity, tokens), 0)
        match = slot == rank[k : k + 1, :]
        onehot[group, pl.ds(local * capacity, capacity), :] = jnp.where(match, 1.0, 0.0).astype(
            jnp.bfloat16
        )
        value = jnp.sum(jnp.where(match, picked[k], 0.0), axis=1, keepdims=True)
        slot_weight[group, pl.ds(local * capacity, capacity), :] = jnp.broadcast_to(
            value, (capacity, LANES)
        )

    pl.semaphore_wait(barrier, groups + half - 1)
    load_cot.wait()

    def exchange(c, j):
        return pltpu.make_async_remote_copy(
            src_ref=send.at[c, j - 1],
            dst_ref=recv.at[c, s],
            send_sem=send_sem.at[c, j - 1],
            recv_sem=recv_sem.at[c, j - 1],
            device_id=(d, lax.rem(s + j, groups)),
            device_id_type=MESH,
        )

    def pair(c):
        return pltpu.make_async_remote_copy(
            src_ref=part.at[c, 1 - parity],
            dst_ref=pair_recv.at[c],
            send_sem=pair_sem.at[c, 0],
            recv_sem=pair_sem.at[c, 1],
            device_id=(partner, s),
            device_id_type=MESH,
        )

    def peer(c, j):
        to = lax.rem(q + j, half)
        return pltpu.make_async_remote_copy(
            src_ref=part.at[c, parity, to],
            dst_ref=peer_recv.at[c, j - 1],
            send_sem=peer_send_sem.at[c, j - 1],
            recv_sem=peer_recv_sem.at[c, j - 1],
            device_id=(to * 2 + parity, s),
            device_id_type=MESH,
        )

    order = sorted(range(1, groups), key=lambda j: abs(j - groups / 2)) + [0]

    def dispatch(c, carry):
        columns = cot[:, pl.ds(pl.multiple_of(c * width, width), width)]
        for j in order:
            group = lax.rem(s + j, groups)
            taken = jnp.dot(onehot[group], columns, preferred_element_type=jnp.float32)
            block = (taken * slot_weight[group][:, :1]).astype(jnp.bfloat16)
            block = block.reshape(local_count, capacity, width)
            if j:
                send[c, j - 1] = block
                exchange(c, j).start()
            else:
                recv[c, s] = block
        return carry

    lax.fori_loop(0, chunks, dispatch, 0)

    load_hidden.wait()
    for local in range(local_count):

        def turn(i, carry, local=local):
            at = pl.ds(pl.multiple_of(i * LANES, LANES), LANES)
            turned[local, at, :] = hidden[local, :, at].T
            return carry

        lax.fori_loop(0, hidden_units // LANES, turn, 0)

    def finish(c):
        total = own_sum[...]
        for j in range(1, half):
            peer(c, j).wait_recv()
            total = total + peer_recv[c, j - 1].astype(jnp.float32)
        grad_ref[:, :, pl.ds(pl.multiple_of(c * width, width), width)] = total

    def step(c, carry):
        for j in range(1, groups):
            exchange(c, j).wait_recv()
        for local in range(local_count):
            held = recv[c, :, local].reshape(rows, width)
            product = jnp.dot(turned[local], held, preferred_element_type=jnp.float32)
            for block in range(dp):
                part[c, block % 2, block // 2, local] = product[
                    block * own : (block + 1) * own
                ].astype(jnp.bfloat16)
        pair(c).start()

        @pl.when(c > 0)
        def _():
            finish(c - 1)

        pair(c).wait_recv()
        for j in list(range(1, half)) + [0]:
            to = lax.rem(q + j, half)
            both = part[c, parity, to].astype(jnp.float32) + pair_recv[c, to].astype(jnp.float32)
            if j:
                part[c, parity, to] = both.astype(jnp.bfloat16)
                peer(c, j).start()
            else:
                own_sum[...] = both
        return carry

    lax.fori_loop(0, chunks, step, 0)
    finish(chunks - 1)

    def drain(c, carry):
        for j in range(1, groups):
            exchange(c, j).wait_send()
        pair(c).wait_send()
        for j in range(1, half):
            peer(c, j).wait_send()
        return carry

    lax.fori_loop(0, chunks, drain, 0)


def gradient_sum(dp, groups, cotangent, route_ids, route_weights, hidden, own):
    tokens, depth = cotangent.shape
    local_count, rows, hidden_units = hidden.shape
    capacity = rows // groups
    window = local_count * groups
    chunks = depth // CHUNK
    half = dp // 2
    top = route_ids.shape[1]
    vmem = pl.BlockSpec(memory_space=pltpu.VMEM)
    anywhere = pl.BlockSpec(memory_space=pl.ANY)
    dma = pltpu.SemaphoreType.DMA
    return pl.pallas_call(
        functools.partial(gradient_kernel, dp, groups),
        out_shape=jax.ShapeDtypeStruct((local_count, own, depth), jnp.float32),
        in_specs=[vmem, vmem, anywhere, anywhere],
        out_specs=vmem,
        scratch_shapes=[
            pltpu.VMEM((tokens, depth), jnp.bfloat16),
            pltpu.VMEM(hidden.shape, jnp.bfloat16),
            pltpu.VMEM((local_count, hidden_units, rows), jnp.bfloat16),
            pltpu.VMEM((groups, local_count * capacity, tokens), jnp.bfloat16),
            pltpu.VMEM((groups, local_count * capacity, LANES), jnp.float32),
            pltpu.VMEM((chunks, groups - 1, local_count, capacity, CHUNK), jnp.bfloat16),
            pltpu.VMEM((chunks, groups, local_count, capacity, CHUNK), jnp.bfloat16),
            pltpu.VMEM((chunks, 2, half, local_count, own, CHUNK), jnp.bfloat16),
            pltpu.VMEM((chunks, half, local_count, own, CHUNK), jnp.bfloat16),
            pltpu.VMEM((chunks, half - 1, local_count, own, CHUNK), jnp.bfloat16),
            pltpu.VMEM((local_count, own, CHUNK), jnp.float32),
            dma((2,)),
            dma((chunks, groups - 1)),
            dma((chunks, groups - 1)),
            dma((chunks, 2)),
            dma((chunks, half - 1)),
            dma((chunks, half - 1)),
        ],
        compiler_params=pltpu.CompilerParams(
            collective_id=0, has_side_effects=True, vmem_limit_bytes=64 * 1024 * 1024 - 65536
        ),
    )(route_ids.T, route_weights.T, cotangent, hidden)


def solution(mesh):
    dp, groups = mesh.shape["dp"], mesh.shape["expert"]

    def shards(cotangent, route_ids, route_weights, hidden, master, first_moment, second_moment):
        capacity = hidden.shape[1] // groups
        summed = gradient_sum(
            dp, groups, cotangent, route_ids, route_weights, hidden, master.shape[0]
        )
        gradient = summed.transpose(1, 0, 2) / jnp.sqrt(jnp.float32(groups * capacity))
        new_first = beta_one * first_moment + (1.0 - beta_one) * gradient
        new_second = beta_two * second_moment + (1.0 - beta_two) * gradient * gradient
        corrected_first = new_first / (1.0 - beta_one**step_count)
        corrected_second = new_second / (1.0 - beta_two**step_count)
        update = corrected_first / (jnp.sqrt(corrected_second) + epsilon) + decay_rate * master
        new_master = master - learning_rate * update
        return (new_master, new_first, new_second)

    placed = (
        P(("dp", "expert"), None),
        P(("dp", "expert"), None),
        P(("dp", "expert"), None),
        P("expert", "dp", None),
        P("dp", "expert", None),
        P("dp", "expert", None),
        P("dp", "expert", None),
    )
    return jax.shard_map(
        shards,
        mesh=mesh,
        in_specs=placed,
        out_specs=(P("dp", "expert", None), P("dp", "expert", None), P("dp", "expert", None)),
        check_vma=False,
    )
```

time: 475 us -> 183 us (0.39)
  Pallas kernels: 0 us -> 159 us
  waiting for transfers between devices: 152 us -> 0 us
  blocking collectives: 144 us -> 0 us
  local copies, waits for them, and re-layouts: 122 us -> 11.4 us
  matrix products: 22.2 us -> 0 us
  between operations: 14.2 us -> 0.65 us
  other arithmetic: 18.9 us -> 10.1 us
    pallas_call x0 -> x1, Pallas kernels: none -> 159 us  [gradient_sum(): pl.pallas_call(functools.partial(gradient_kernel, dp, groups), out_shape=...]
    reduce_scatter x2 -> x0, waiting for transfers between devices: 152 us -> none  [shards(): lax.psum_scatter(one_term(jnp.int32(0), owned_rows * lax.axis_size('dp'))...]
    all_to_all x1 -> x0, blocking collectives: 144 us -> none  [shards(): lax.all_to_all(scaled, 'expert', split_axis=1, concat_axis=1, tiled=True)]
    scatter x2 -> x0, local copies, waits for them, and re-layouts: 46 us -> none  [the longest x1 23 us: slot_table(): slot_weight = jnp.zeros((window * capacity + 1,), route_weights.dtype).at...]
    unnamed x11 -> x3, local copies, waits for them, and re-layouts: 36.2 us -> 11.4 us
    dot_general x2 -> x0, matrix products: 22.2 us -> none  [one_term(): jnp.einsum('rf,rd->fd', hidden_one, received_one, preferred_element_type=...]
    gather x1 -> x0, local copies, waits for them, and re-layouts: 15.5 us -> none  [shards(): cotangent[slot_anchor].astype(jnp.float32) * slot_weight[:, None]]
    convert_element_type x1 -> x0, local copies, waits for them, and re-layouts: 13 us -> none  [shards(): (cotangent[slot_anchor].astype(jnp.float32) * slot_weight[:, None]).astyp...]
  transfers between devices with their start and end apart: 2 -> 0, of which waited for: 2 -> 0; matrix products, arithmetic and copies ran while one was open for 5% -> 0% of each run, Pallas kernels for 0% -> 0%
where the time goes in v1:
time: 183 us; the launch traced here: 181 us
  Pallas kernels  159 us (87%)
  local copies, waits for them, and re-layouts  11.4 us (6%)
  other arithmetic  10.1 us (6%)
    pallas_call x1, Pallas kernels, gradient_sum(): pl.pallas_call(functools.partial(gradient_kernel, dp, groups), out_shape=...  159 us
    unnamed x3, local copies, waits for them, and re-layouts  11.4 us
    sub x1, other arithmetic, shards(): new_master = master - learning_rate * update  10.1 us

profile of v1, /device:TPU:0, one launch (start us, length us, event | category | flops | bytes accessed | tf_op | source)
XLA Modules:
  0.0 180.8 jit_solution(10161820139486823526)
XLA Ops:
  0.6 158.7 %shard_map.94 = f32[2,176,2048]{2,1,0:T(8,128)} custom-call(s32[6,1024]{1,0:T(8,128)} %bitcast.8, f32[6,1024]{1,0:T(8,128)} %bitcast.9, bf16[1024,2048]{1,0:T(8,128)(2,1)} %cot_hbm.1, bf16[2,768,1408]{2,1,0:T(8,128)(2,1)} %hidden_hbm.1), custom_call_target="tpu_custom_call" | custom-call | tf_op jit(solution)/shard_map/pallas_call | solution.py:229
  159.3 10.1 %multiply_subtract_fusion = (f32[176,2,2048]{2,0,1:T(8,128)S(1)}, f32[176,2,2048]{2,0,1:T(8,128)S(1)}, f32[176,2,2048]{2,0,1:T(8,128)S(1)}) fusion(f32[176,2,2048]{2,1,0:T(2,128)} %param.11, f32[2,176,2048]{2,1,0:T(8,128)} %shard_map.94, f32[176,2,2048]{2,1,0:T(2,128)} %param.12, f32[176,2,2048]{2,1,0:T(2,128)} %param.13), kind=kLoop, calls=%fused_computation.4 | loop fusion | flops 11534336 | bytes 20185088 | tf_op jit(solution)/shard_map/sub | solution.py:273
  169.4 3.8 %copy.14 = f32[176,2,2048]{2,1,0:T(2,128)} copy(f32[176,2,2048]{2,0,1:T(8,128)S(1)} %get-tuple-element.6) | data formatting | bytes 5767168
  173.2 3.8 %copy.15 = f32[176,2,2048]{2,1,0:T(2,128)} copy(f32[176,2,2048]{2,0,1:T(8,128)S(1)} %get-tuple-element.7) | data formatting | bytes 5767168
  177.0 3.8 %copy.16 = f32[176,2,2048]{2,1,0:T(2,128)} copy(f32[176,2,2048]{2,0,1:T(8,128)S(1)} %get-tuple-element.8) | data formatting | bytes 5767168

commit v2 on v1

--- a/solution.py
+++ b/solution.py
@@ -16,7 +16,7 @@
 
 MESH = pl.DeviceIdType.MESH
 LANES = 128
-CHUNK = 256
+CHUNK = 128
 
 
 def gradient_kernel(
@@ -55,7 +55,8 @@
     local_count, capacity = recv.shape[2], recv.shape[3]
     top, tokens = ids_ref.shape
     rows = groups * capacity
-    own = grad_ref.shape[1]
+    own = own_sum.shape[1]
+    stride = chunks * (width // LANES) * local_count
     hidden_units = turned.shape[1]
 
     load_cot = pltpu.make_async_copy(cot_hbm, cot, load_sem.at[0])
@@ -120,8 +121,8 @@
 
     def pair(c):
         return pltpu.make_async_remote_copy(
-            src_ref=part.at[c, 1 - parity],
-            dst_ref=pair_recv.at[c],
+            src_ref=part.at[lax.rem(c, 2), 1 - parity],
+            dst_ref=pair_recv.at[lax.rem(c, 2)],
             send_sem=pair_sem.at[c, 0],
             recv_sem=pair_sem.at[c, 1],
             device_id=(partner, s),
@@ -131,8 +132,8 @@
     def peer(c, j):
         to = lax.rem(q + j, half)
         return pltpu.make_async_remote_copy(
-            src_ref=part.at[c, parity, to],
-            dst_ref=peer_recv.at[c, j - 1],
+            src_ref=part.at[lax.rem(c, 2), parity, to],
+            dst_ref=peer_recv.at[lax.rem(c, 2), j - 1],
             send_sem=peer_send_sem.at[c, j - 1],
             recv_sem=peer_recv_sem.at[c, j - 1],
             device_id=(to * 2 + parity, s),
@@ -171,17 +172,33 @@
         total = own_sum[...]
         for j in range(1, half):
             peer(c, j).wait_recv()
-            total = total + peer_recv[c, j - 1].astype(jnp.float32)
-        grad_ref[:, :, pl.ds(pl.multiple_of(c * width, width), width)] = total
+            total = total + peer_recv[lax.rem(c, 2), j - 1].astype(jnp.float32)
+        for local in range(local_count):
+            for tile in range(width // LANES):
+                first = (c * (width // LANES) + tile) * local_count + local
+                grad_ref[pl.ds(first, own, stride=stride), :] = total[
+                    local, :, tile * LANES : (tile + 1) * LANES
+                ]
+
+    def sent(c):
+        pair(c).wait_send()
+        for j in range(1, half):
+            peer(c, j).wait_send()
 
     def step(c, carry):
+        slot = lax.rem(c, 2)
+
+        @pl.when(c > 1)
+        def _():
+            sent(c - 2)
+
         for j in range(1, groups):
             exchange(c, j).wait_recv()
         for local in range(local_count):
             held = recv[c, :, local].reshape(rows, width)
             product = jnp.dot(turned[local], held, preferred_element_type=jnp.float32)
             for block in range(dp):
-                part[c, block % 2, block // 2, local] = product[
+                part[slot, block % 2, block // 2, local] = product[
                     block * own : (block + 1) * own
                 ].astype(jnp.bfloat16)
         pair(c).start()
@@ -193,9 +210,9 @@
         pair(c).wait_recv()
         for j in list(range(1, half)) + [0]:
             to = lax.rem(q + j, half)
-            both = part[c, parity, to].astype(jnp.float32) + pair_recv[c, to].astype(jnp.float32)
+            both = part[slot, parity, to].astype(jnp.float32) + pair_recv[slot, to].astype(jnp.float32)
             if j:
-                part[c, parity, to] = both.astype(jnp.bfloat16)
+                part[slot, parity, to] = both.astype(jnp.bfloat16)
                 peer(c, j).start()
             else:
                 own_sum[...] = both
@@ -207,11 +224,10 @@
     def drain(c, carry):
         for j in range(1, groups):
             exchange(c, j).wait_send()
-        pair(c).wait_send()
-        for j in range(1, half):
-            peer(c, j).wait_send()
         return carry
 
+    for c in range(max(chunks - 2, 0), chunks):
+        sent(c)
     lax.fori_loop(0, chunks, drain, 0)
 
 
@@ -224,11 +240,11 @@
     half = dp // 2
     top = route_ids.shape[1]
     vmem = pl.BlockSpec(memory_space=pltpu.VMEM)
-    anywhere = pl.BlockSpec(memory_space=pl.ANY)
+    anywhere = pl.BlockSpec(memory_space=pltpu.HBM)
     dma = pltpu.SemaphoreType.DMA
     return pl.pallas_call(
         functools.partial(gradient_kernel, dp, groups),
-        out_shape=jax.ShapeDtypeStruct((local_count, own, depth), jnp.float32),
+        out_shape=jax.ShapeDtypeStruct((own * depth * local_count // LANES, LANES), jnp.float32),
         in_specs=[vmem, vmem, anywhere, anywhere],
         out_specs=vmem,
         scratch_shapes=[
@@ -239,9 +255,9 @@
             pltpu.VMEM((groups, local_count * capacity, LANES), jnp.float32),
             pltpu.VMEM((chunks, groups - 1, local_count, capacity, CHUNK), jnp.bfloat16),
             pltpu.VMEM((chunks, groups, local_count, capacity, CHUNK), jnp.bfloat16),
-            pltpu.VMEM((chunks, 2, half, local_count, own, CHUNK), jnp.bfloat16),
-            pltpu.VMEM((chunks, half, local_count, own, CHUNK), jnp.bfloat16),
-            pltpu.VMEM((chunks, half - 1, local_count, own, CHUNK), jnp.bfloat16),
+            pltpu.VMEM((2, 2, half, local_count, own, CHUNK), jnp.bfloat16),
+            pltpu.VMEM((2, half, local_count, own, CHUNK), jnp.bfloat16),
+            pltpu.VMEM((2, half - 1, local_count, own, CHUNK), jnp.bfloat16),
             pltpu.VMEM((local_count, own, CHUNK), jnp.float32),
             dma((2,)),
             dma((chunks, groups - 1)),
@@ -251,7 +267,7 @@
             dma((chunks, half - 1)),
         ],
         compiler_params=pltpu.CompilerParams(
-            collective_id=0, has_side_effects=True, vmem_limit_bytes=64 * 1024 * 1024 - 65536
+            collective_id=0, has_side_effects=True, vmem_limit_bytes=44 * 1024 * 1024
         ),
     )(route_ids.T, route_weights.T, cotangent, hidden)
 
@@ -264,14 +280,26 @@
         summed = gradient_sum(
             dp, groups, cotangent, route_ids, route_weights, hidden, master.shape[0]
         )
-        gradient = summed.transpose(1, 0, 2) / jnp.sqrt(jnp.float32(groups * capacity))
+        shape = master.shape
+        split = (shape[0], shape[1], shape[2] // LANES, LANES)
+
+        def flat(x):
+            return x.reshape(split).transpose(0, 2, 1, 3).reshape(-1, LANES)
+
+        def whole(x):
+            return x.reshape(split[0], split[2], split[1], LANES).transpose(0, 2, 1, 3).reshape(shape)
+
+        master, first_moment, second_moment = lax.optimization_barrier(
+            (flat(master), flat(first_moment), flat(second_moment))
+        )
+        gradient = summed / jnp.sqrt(jnp.float32(groups * capacity))
         new_first = beta_one * first_moment + (1.0 - beta_one) * gradient
         new_second = beta_two * second_moment + (1.0 - beta_two) * gradient * gradient
         corrected_first = new_first / (1.0 - beta_one**step_count)
         corrected_second = new_second / (1.0 - beta_two**step_count)
         update = corrected_first / (jnp.sqrt(corrected_second) + epsilon) + decay_rate * master
         new_master = master - learning_rate * update
-        return (new_master, new_first, new_second)
+        return (whole(new_master), whole(new_first), whole(new_second))
 
     placed = (
         P(("dp", "expert"), None),

time: 183 us -> 172 us (0.940)
  local copies, waits for them, and re-layouts: 11.4 us -> 3.71 us
  other arithmetic: 10.1 us -> 4.15 us
    unnamed x3 -> x12, local copies, waits for them, and re-layouts: 11.4 us -> 3.71 us
    sub x1, other arithmetic: 10.1 us -> 4.15 us  [shards(): new_master = master - learning_rate * update]
where the time goes in v2:
time: 172 us; the launch traced here: 169 us
  Pallas kernels  160 us (93%)
  other arithmetic  4.15 us (2%)
  local copies, waits for them, and re-layouts  3.71 us (2%)
    pallas_call x1, Pallas kernels, gradient_sum(): pl.pallas_call(functools.partial(gradient_kernel, dp, groups), out_shape=...  160 us
    sub x1, other arithmetic, shards(): new_master = master - learning_rate * update  4.15 us
    unnamed x12, local copies, waits for them, and re-layouts  3.71 us

profile of v2, /device:TPU:0, one launch (start us, length us, event | category | flops | bytes accessed | tf_op | source)
XLA Modules:
  0.0 168.9 jit_solution(5348904219600649955)
XLA Ops:
  0.6 0.0 copy-start
  0.6 2.2 %copy-done = bf16[1024,2048]{1,0:T(8,128)(2,1)S(1)} copy-done((bf16[1024,2048]{1,0:T(8,128)(2,1)S(1)}, bf16[1024,2048]{1,0:T(8,128)(2,1)}, u32[]{:S(2)}) %copy-start) | copy-done | bytes 4194328
  2.8 0.0 copy-start.1
  2.8 0.8 copy-done.1
  3.6 0.0 copy-start.2
  3.6 0.8 copy-done.2
  4.3 0.0 copy-start.3
  4.3 0.0 copy-start.4
  4.3 0.0 copy-start.5
  4.3 160.4 %shard_map.94 = f32[5632,128]{1,0:T(8,128)S(1)} custom-call(s32[6,1024]{1,0:T(8,128)S(1)} %bitcast.32, f32[6,1024]{1,0:T(8,128)S(1)} %bitcast.33, bf16[1024,2048]{1,0:T(8,128)(2,1)S(1)} %copy-done, bf16[2,768,1408]{2,1,0:T(8,128)(2,1)} %hidden_hbm.1), custom_call_target="tpu_custom_call" | custom-call | tf_op jit(solution)/shard_map/pallas_call | solution.py:245
  164.7 0.0 copy-done.3
  164.7 0.0 copy-done.4
  164.7 0.0 copy-done.5
  164.7 4.2 %multiply_subtract_fusion = (f32[5632,128]{1,0:T(8,128)}, f32[5632,128]{1,0:T(8,128)}, f32[5632,128]{1,0:T(8,128)}) fusion(f32[5632,128]{1,0:T(8,128)S(1)} %bitcast.34, f32[5632,128]{1,0:T(8,128)S(1)} %shard_map.94, f32[5632,128]{1,0:T(8,128)S(1)} %bitcast.35, f32[5632,128]{1,0:T(8,128)S(1)} %bitcast.36), kind=kLoop, calls=%fused_computation | loop fusion | flops 11534336 | bytes 20185088 | tf_op jit(solution)/shard_map/sub | solution.py:301
Async XLA Ops:
  0.6 2.2 %copy-start = (bf16[1024,2048]{1,0:T(8,128)(2,1)S(1)}, bf16[1024,2048]{1,0:T(8,128)(2,1)}, u32[]{:S(2)}) copy-start(bf16[1024,2048]{1,0:T(8,128)(2,1)} %cot_hbm.1) | copy-start | bytes 12582916
  2.8 0.8 copy-start.1
  3.6 0.8 copy-start.2
  4.3 160.4 %copy-start.3 = (f32[176,2,2048]{2,1,0:T(2,128)S(1)}, f32[176,2,2048]{2,1,0:T(2,128)}, u32[]{:S(2)}) copy-start(f32[176,2,2048]{2,1,0:T(2,128)} %param.11) | copy-start | bytes 8650756
  4.3 160.4 %copy-start.4 = (f32[176,2,2048]{2,1,0:T(2,128)S(1)}, f32[176,2,2048]{2,1,0:T(2,128)}, u32[]{:S(2)}) copy-start(f32[176,2,2048]{2,1,0:T(2,128)} %param.12) | copy-start | bytes 8650756
  4.3 160.4 %copy-start.5 = (f32[176,2,2048]{2,1,0:T(2,128)S(1)}, f32[176,2,2048]{2,1,0:T(2,128)}, u32[]{:S(2)}) copy-start(f32[176,2,2048]{2,1,0:T(2,128)} %param.13) | copy-start | bytes 8650756

commit v3 on v2

--- a/solution.py
+++ b/solution.py
@@ -17,6 +17,7 @@
 MESH = pl.DeviceIdType.MESH
 LANES = 128
 CHUNK = 128
+SLOTS = 4
 
 
 def gradient_kernel(
@@ -55,7 +56,7 @@
     local_count, capacity = recv.shape[2], recv.shape[3]
     top, tokens = ids_ref.shape
     rows = groups * capacity
-    own = own_sum.shape[1]
+    own = own_sum.shape[2]
     stride = chunks * (width // LANES) * local_count
     hidden_units = turned.shape[1]
 
@@ -121,8 +122,8 @@
 
     def pair(c):
         return pltpu.make_async_remote_copy(
-            src_ref=part.at[lax.rem(c, 2), 1 - parity],
-            dst_ref=pair_recv.at[lax.rem(c, 2)],
+            src_ref=part.at[lax.rem(c, SLOTS), 1 - parity],
+            dst_ref=pair_recv.at[lax.rem(c, SLOTS)],
             send_sem=pair_sem.at[c, 0],
             recv_sem=pair_sem.at[c, 1],
             device_id=(partner, s),
@@ -132,8 +133,8 @@
     def peer(c, j):
         to = lax.rem(q + j, half)
         return pltpu.make_async_remote_copy(
-            src_ref=part.at[lax.rem(c, 2), parity, to],
-            dst_ref=peer_recv.at[lax.rem(c, 2), j - 1],
+            src_ref=part.at[lax.rem(c, SLOTS), parity, to],
+            dst_ref=peer_recv.at[lax.rem(c, SLOTS), j - 1],
             send_sem=peer_send_sem.at[c, j - 1],
             recv_sem=peer_recv_sem.at[c, j - 1],
             device_id=(to * 2 + parity, s),
@@ -169,10 +170,10 @@
         lax.fori_loop(0, hidden_units // LANES, turn, 0)
 
     def finish(c):
-        total = own_sum[...]
+        total = own_sum[lax.rem(c, SLOTS)]
         for j in range(1, half):
             peer(c, j).wait_recv()
-            total = total + peer_recv[lax.rem(c, 2), j - 1].astype(jnp.float32)
+            total = total + peer_recv[lax.rem(c, SLOTS), j - 1].astype(jnp.float32)
         for local in range(local_count):
             for tile in range(width // LANES):
                 first = (c * (width // LANES) + tile) * local_count + local
@@ -180,17 +181,31 @@
                     local, :, tile * LANES : (tile + 1) * LANES
                 ]
 
+    def combine(c):
+        slot = lax.rem(c, SLOTS)
+        pair(c).wait_recv()
+        for j in list(range(1, half)) + [0]:
+            to = lax.rem(q + j, half)
+            both = part[slot, parity, to].astype(jnp.float32) + pair_recv[slot, to].astype(
+                jnp.float32
+            )
+            if j:
+                part[slot, parity, to] = both.astype(jnp.bfloat16)
+                peer(c, j).start()
+            else:
+                own_sum[slot] = both
+
     def sent(c):
         pair(c).wait_send()
         for j in range(1, half):
             peer(c, j).wait_send()
 
     def step(c, carry):
-        slot = lax.rem(c, 2)
-
-        @pl.when(c > 1)
+        slot = lax.rem(c, SLOTS)
+
+        @pl.when(c >= SLOTS)
         def _():
-            sent(c - 2)
+            sent(c - SLOTS)
 
         for j in range(1, groups):
             exchange(c, j).wait_recv()
@@ -205,20 +220,18 @@
 
         @pl.when(c > 0)
         def _():
-            finish(c - 1)
-
-        pair(c).wait_recv()
-        for j in list(range(1, half)) + [0]:
-            to = lax.rem(q + j, half)
-            both = part[slot, parity, to].astype(jnp.float32) + pair_recv[slot, to].astype(jnp.float32)
-            if j:
-                part[slot, parity, to] = both.astype(jnp.bfloat16)
-                peer(c, j).start()
-            else:
-                own_sum[...] = both
+            combine(c - 1)
+
+        @pl.when(c > 1)
+        def _():
+            finish(c - 2)
+
         return carry
 
     lax.fori_loop(0, chunks, step, 0)
+    combine(chunks - 1)
+    if chunks > 1:
+        finish(chunks - 2)
     finish(chunks - 1)
 
     def drain(c, carry):
@@ -226,7 +239,7 @@
             exchange(c, j).wait_send()
         return carry
 
-    for c in range(max(chunks - 2, 0), chunks):
+    for c in range(max(chunks - SLOTS, 0), chunks):
         sent(c)
     lax.fori_loop(0, chunks, drain, 0)
 
@@ -255,10 +268,10 @@
             pltpu.VMEM((groups, local_count * capacity, LANES), jnp.float32),
             pltpu.VMEM((chunks, groups - 1, local_count, capacity, CHUNK), jnp.bfloat16),
             pltpu.VMEM((chunks, groups, local_count, capacity, CHUNK), jnp.bfloat16),
-            pltpu.VMEM((2, 2, half, local_count, own, CHUNK), jnp.bfloat16),
-            pltpu.VMEM((2, half, local_count, own, CHUNK), jnp.bfloat16),
-            pltpu.VMEM((2, half - 1, local_count, own, CHUNK), jnp.bfloat16),
-            pltpu.VMEM((local_count, own, CHUNK), jnp.float32),
+            pltpu.VMEM((SLOTS, 2, half, local_count, own, CHUNK), jnp.bfloat16),
+            pltpu.VMEM((SLOTS, half, local_count, own, CHUNK), jnp.bfloat16),
+            pltpu.VMEM((SLOTS, half - 1, local_count, own, CHUNK), jnp.bfloat16),
+            pltpu.VMEM((SLOTS, local_count, own, CHUNK), jnp.float32),
             dma((2,)),
             dma((chunks, groups - 1)),
             dma((chunks, groups - 1)),
@@ -267,7 +280,7 @@
             dma((chunks, half - 1)),
         ],
         compiler_params=pltpu.CompilerParams(
-            collective_id=0, has_side_effects=True, vmem_limit_bytes=44 * 1024 * 1024
+            collective_id=0, has_side_effects=True, vmem_limit_bytes=50 * 1024 * 1024
         ),
     )(route_ids.T, route_weights.T, cotangent, hidden)
 

time: 172 us -> 160 us (0.930); the launches traced: 169 us -> 160 us
  Pallas kernels: 160 us -> 154 us
  local copies, waits for them, and re-layouts: 3.71 us -> 1.52 us
    pallas_call x1, Pallas kernels: 160 us -> 154 us  [gradient_sum(): pl.pallas_call(functools.partial(gradient_kernel, dp, groups), out_shape=...]
    unnamed x12 -> x10, local copies, waits for them, and re-layouts: 3.71 us -> 1.52 us
where the time goes in v3:
time: 160 us
  Pallas kernels  154 us (96%)
  other arithmetic  4.15 us (3%)
    pallas_call x1, Pallas kernels, gradient_sum(): pl.pallas_call(functools.partial(gradient_kernel, dp, groups), out_shape=...  154 us
    sub x1, other arithmetic, shards(): new_master = master - learning_rate * update  4.15 us

profile of v3, /device:TPU:0, one launch (start us, length us, event | category | flops | bytes accessed | tf_op | source)
XLA Modules:
  0.0 160.1 jit_solution(9543845746563756726)
XLA Ops:
  0.6 0.0 copy-start
  0.6 0.7 copy-done
  1.4 0.0 copy-start.1
  1.4 0.8 copy-done.1
  2.1 0.0 copy-start.2
  2.2 0.0 copy-start.3
  2.2 0.0 copy-start.4
  2.2 153.8 %shard_map.94 = f32[5632,128]{1,0:T(8,128)S(1)} custom-call(s32[6,1024]{1,0:T(8,128)S(1)} %bitcast.32, f32[6,1024]{1,0:T(8,128)S(1)} %bitcast.33, bf16[1024,2048]{1,0:T(8,128)(2,1)} %cot_hbm.1, bf16[2,768,1408]{2,1,0:T(8,128)(2,1)} %hidden_hbm.1), custom_call_target="tpu_custom_call" | custom-call | tf_op jit(solution)/shard_map/pallas_call | solution.py:258
  155.9 0.0 copy-done.2
  155.9 0.0 copy-done.3
  156.0 0.0 copy-done.4
  156.0 4.2 %multiply_subtract_fusion = (f32[5632,128]{1,0:T(8,128)}, f32[5632,128]{1,0:T(8,128)}, f32[5632,128]{1,0:T(8,128)}) fusion(f32[5632,128]{1,0:T(8,128)S(1)} %bitcast.34, f32[5632,128]{1,0:T(8,128)S(1)} %shard_map.94, f32[5632,128]{1,0:T(8,128)S(1)} %bitcast.35, f32[5632,128]{1,0:T(8,128)S(1)} %bitcast.36), kind=kLoop, calls=%fused_computation | loop fusion | flops 11534336 | bytes 20185088 | tf_op jit(solution)/shard_map/sub | solution.py:314
Async XLA Ops:
  0.6 0.8 copy-start
  1.4 0.8 copy-start.1
  2.1 153.8 %copy-start.2 = (f32[176,2,2048]{2,1,0:T(2,128)S(1)}, f32[176,2,2048]{2,1,0:T(2,128)}, u32[]{:S(2)}) copy-start(f32[176,2,2048]{2,1,0:T(2,128)} %param.11) | copy-start | bytes 8650756
  2.2 153.8 %copy-start.3 = (f32[176,2,2048]{2,1,0:T(2,128)S(1)}, f32[176,2,2048]{2,1,0:T(2,128)}, u32[]{:S(2)}) copy-start(f32[176,2,2048]{2,1,0:T(2,128)} %param.12) | copy-start | bytes 8650756
  2.2 153.8 %copy-start.4 = (f32[176,2,2048]{2,1,0:T(2,128)S(1)}, f32[176,2,2048]{2,1,0:T(2,128)}, u32[]{:S(2)}) copy-start(f32[176,2,2048]{2,1,0:T(2,128)} %param.13) | copy-start | bytes 8650756

commit v4 on v3

--- a/solution.py
+++ b/solution.py
@@ -141,20 +141,26 @@
             device_id_type=MESH,
         )
 
-    order = sorted(range(1, groups), key=lambda j: abs(j - groups / 2)) + [0]
+    upper = s * 2 // groups
+    late = list(range(1, groups))
+    early = late[1:2] + late[:1] + late[2:]
+    order = []
+    for first, second in zip(early, late):
+        j = first + (second - first) * parity
+        order.append(j + (groups - 2 * j) * upper)
 
     def dispatch(c, carry):
         columns = cot[:, pl.ds(pl.multiple_of(c * width, width), width)]
-        for j in order:
-            group = lax.rem(s + j, groups)
+        for j in order + [None]:
+            group = s if j is None else lax.rem(s + j, groups)
             taken = jnp.dot(onehot[group], columns, preferred_element_type=jnp.float32)
             block = (taken * slot_weight[group][:, :1]).astype(jnp.bfloat16)
             block = block.reshape(local_count, capacity, width)
-            if j:
+            if j is None:
+                recv[c, s] = block
+            else:
                 send[c, j - 1] = block
                 exchange(c, j).start()
-            else:
-                recv[c, s] = block
         return carry
 
     lax.fori_loop(0, chunks, dispatch, 0)

time: 160 us -> 162 us (1.012)
  Pallas kernels: 154 us -> 156 us
    pallas_call x1, Pallas kernels: 154 us -> 156 us  [gradient_sum(): pl.pallas_call(functools.partial(gradient_kernel, dp, groups), out_shape=...]
where the time goes in v4:
time: 162 us
  Pallas kernels  156 us (96%)
  other arithmetic  4.15 us (3%)
    pallas_call x1, Pallas kernels, gradient_sum(): pl.pallas_call(functools.partial(gradient_kernel, dp, groups), out_shape=...  156 us
    sub x1, other arithmetic, shards(): new_master = master - learning_rate * update  4.15 us

profile of v4, /device:TPU:0, one launch (start us, length us, event | category | flops | bytes accessed | tf_op | source)
XLA Modules:
  0.0 162.1 jit_solution(638479196459833118)
XLA Ops:
  0.6 0.0 copy-start
  0.6 0.7 copy-done
  1.4 0.0 copy-start.1
  1.4 0.8 copy-done.1
  2.1 0.0 copy-start.2
  2.2 0.0 copy-start.3
  2.2 0.0 copy-start.4
  2.2 155.8 %shard_map.94 = f32[5632,128]{1,0:T(8,128)S(1)} custom-call(s32[6,1024]{1,0:T(8,128)S(1)} %bitcast.32, f32[6,1024]{1,0:T(8,128)S(1)} %bitcast.33, bf16[1024,2048]{1,0:T(8,128)(2,1)} %cot_hbm.1, bf16[2,768,1408]{2,1,0:T(8,128)(2,1)} %hidden_hbm.1), custom_call_target="tpu_custom_call" | custom-call | tf_op jit(solution)/shard_map/pallas_call | solution.py:264
  157.9 0.0 copy-done.2
  157.9 0.0 copy-done.3
  157.9 0.0 copy-done.4
  158.0 4.2 %multiply_subtract_fusion = (f32[5632,128]{1,0:T(8,128)}, f32[5632,128]{1,0:T(8,128)}, f32[5632,128]{1,0:T(8,128)}) fusion(f32[5632,128]{1,0:T(8,128)S(1)} %bitcast.34, f32[5632,128]{1,0:T(8,128)S(1)} %shard_map.94, f32[5632,128]{1,0:T(8,128)S(1)} %bitcast.35, f32[5632,128]{1,0:T(8,128)S(1)} %bitcast.36), kind=kLoop, calls=%fused_computation | loop fusion | flops 11534336 | bytes 20185088 | tf_op jit(solution)/shard_map/sub | solution.py:320
Async XLA Ops:
  0.6 0.8 copy-start
  1.4 0.8 copy-start.1
  2.1 155.8 %copy-start.2 = (f32[176,2,2048]{2,1,0:T(2,128)S(1)}, f32[176,2,2048]{2,1,0:T(2,128)}, u32[]{:S(2)}) copy-start(f32[176,2,2048]{2,1,0:T(2,128)} %param.11) | copy-start | bytes 8650756
  2.2 155.8 %copy-start.3 = (f32[176,2,2048]{2,1,0:T(2,128)S(1)}, f32[176,2,2048]{2,1,0:T(2,128)}, u32[]{:S(2)}) copy-start(f32[176,2,2048]{2,1,0:T(2,128)} %param.12) | copy-start | bytes 8650756
  2.2 155.8 %copy-start.4 = (f32[176,2,2048]{2,1,0:T(2,128)S(1)}, f32[176,2,2048]{2,1,0:T(2,128)}, u32[]{:S(2)}) copy-start(f32[176,2,2048]{2,1,0:T(2,128)} %param.13) | copy-start | bytes 8650756

commit v5 on v3

--- a/solution.py
+++ b/solution.py
@@ -200,7 +200,18 @@
         for j in range(1, half):
             peer(c, j).wait_send()
 
-    def step(c, carry):
+    def behind(c):
+        @pl.when(c > 0)
+        def _():
+            combine(c - 1)
+
+        @pl.when(c > 1)
+        def _():
+            finish(c - 2)
+
+    def step(ahead, c, carry):
+        if ahead:
+            behind(c)
         slot = lax.rem(c, SLOTS)
 
         @pl.when(c >= SLOTS)
@@ -218,17 +229,13 @@
                 ].astype(jnp.bfloat16)
         pair(c).start()
 
-        @pl.when(c > 0)
-        def _():
-            combine(c - 1)
-
-        @pl.when(c > 1)
-        def _():
-            finish(c - 2)
-
+        if not ahead:
+            behind(c)
         return carry
 
-    lax.fori_loop(0, chunks, step, 0)
+    turn_at = chunks * 3 // 4
+    lax.fori_loop(0, turn_at, functools.partial(step, False), 0)
+    lax.fori_loop(turn_at, chunks, functools.partial(step, True), 0)
     combine(chunks - 1)
     if chunks > 1:
         finish(chunks - 2)

time: 160 us -> 162 us (1.012)
  no operation moved by 1% of the time
where the time goes in v5:
time: 162 us; the launch traced here: 161 us
  Pallas kernels  155 us (96%)
  other arithmetic  4.15 us (3%)
    pallas_call x1, Pallas kernels, gradient_sum(): pl.pallas_call(functools.partial(gradient_kernel, dp, groups), out_shape=...  155 us
    sub x1, other arithmetic, shards(): new_master = master - learning_rate * update  4.15 us

profile of v5, /device:TPU:0, one launch (start us, length us, event | category | flops | bytes accessed | tf_op | source)
XLA Modules:
  0.0 161.3 jit_solution(17646781721857928256)
XLA Ops:
  0.6 0.0 copy-start
  0.6 0.7 copy-done
  1.4 0.0 copy-start.1
  1.4 0.8 copy-done.1
  2.1 0.0 copy-start.2
  2.2 0.0 copy-start.3
  2.2 0.0 copy-start.4
  2.2 154.9 %shard_map.94 = f32[5632,128]{1,0:T(8,128)S(1)} custom-call(s32[6,1024]{1,0:T(8,128)S(1)} %bitcast.32, f32[6,1024]{1,0:T(8,128)S(1)} %bitcast.33, bf16[1024,2048]{1,0:T(8,128)(2,1)} %cot_hbm.1, bf16[2,768,1408]{2,1,0:T(8,128)(2,1)} %hidden_hbm.1), custom_call_target="tpu_custom_call" | custom-call | tf_op jit(solution)/shard_map/pallas_call | solution.py:265
  157.1 0.0 copy-done.2
  157.1 0.0 copy-done.3
  157.1 0.0 copy-done.4
  157.1 4.2 %multiply_subtract_fusion = (f32[5632,128]{1,0:T(8,128)}, f32[5632,128]{1,0:T(8,128)}, f32[5632,128]{1,0:T(8,128)}) fusion(f32[5632,128]{1,0:T(8,128)S(1)} %bitcast.34, f32[5632,128]{1,0:T(8,128)S(1)} %shard_map.94, f32[5632,128]{1,0:T(8,128)S(1)} %bitcast.35, f32[5632,128]{1,0:T(8,128)S(1)} %bitcast.36), kind=kLoop, calls=%fused_computation | loop fusion | flops 11534336 | bytes 20185088 | tf_op jit(solution)/shard_map/sub | solution.py:321
Async XLA Ops:
  0.6 0.8 copy-start
  1.4 0.8 copy-start.1
  2.1 155.0 %copy-start.2 = (f32[176,2,2048]{2,1,0:T(2,128)S(1)}, f32[176,2,2048]{2,1,0:T(2,128)}, u32[]{:S(2)}) copy-start(f32[176,2,2048]{2,1,0:T(2,128)} %param.11) | copy-start | bytes 8650756
  2.2 155.0 %copy-start.3 = (f32[176,2,2048]{2,1,0:T(2,128)S(1)}, f32[176,2,2048]{2,1,0:T(2,128)}, u32[]{:S(2)}) copy-start(f32[176,2,2048]{2,1,0:T(2,128)} %param.12) | copy-start | bytes 8650756
  2.2 155.0 %copy-start.4 = (f32[176,2,2048]{2,1,0:T(2,128)S(1)}, f32[176,2,2048]{2,1,0:T(2,128)}, u32[]{:S(2)}) copy-start(f32[176,2,2048]{2,1,0:T(2,128)} %param.13) | copy-start | bytes 8650756
